TPU v7x, 256 devices: a whole 4x4x8 slice. The times are simulated.
256 devices in a mesh: row: 32 (over y, z_lo, core), col: 8 (over x, z_hi).
Axes of the slice: x: 4, y: 4, z: 8 (z_hi: 2, z_lo: 4; z = z_hi * 4 + z_lo), core: 2. Of those that a mesh axis runs over, the one named last changes fastest.
Arguments:
- features: bfloat16 [32768, 512], P(('row', 'col')), may hold values from -6 to 6
- edge_tiles: bfloat16 [8192, 128, 128], P(('row', 'col')), may hold values from 0 to 1
- tile_rows: int32 [256, 32], P(('row', 'col')), may hold values from 0 to 7
- tile_cols: int32 [256, 32], P(('row', 'col')), may hold values from 0 to 31
- tile_count: int32 [256], P(('row', 'col')), may hold values from 8 to 32, as said below
- node_order: int32 [256, 128], P(('row', 'col')), may hold values from 0 to 127, each once within a row
- w_self: bfloat16 [512, 512], replicated, may hold values from -0.25 to 0.25
- w_neigh: bfloat16 [512, 512], replicated, may hold values from -12 to 12
- bias_term: bfloat16 [512], replicated, may hold values from -3 to 3
- cotangent: bfloat16 [32768, 512], P(('row', 'col')), may hold values from -6 to 6
Outputs:
- activations: bfloat16 [32768, 512], P(('row', 'col'))
- feature_grad: float32 [32768, 512], P(('row', 'col'))
- self_grad: float32 [512, 512], replicated
- neigh_grad: float32 [512, 512], replicated
- bias_grad: float32 [512], replicated
Inputs may be any that keep to these rules, and one draw needn't show every extreme that they name: Only the first tile_count[b] slots of block b's tile list are valid; later slots are padding and are ignored. The busiest block holds 32 tiles and the lightest 32 // 4. `tile_rows`: tile coordinates may repeat within a block's list. `tile_cols`: tile coordinates may repeat within a block's list.
All inputs are finite; a program needn't handle non-finite values.
Results may differ from a plain program's by a relative error of at most 0.0042.
Values may be sent and summed in bfloat16 or wider, within the bound.
A program may use at most 64 MiB of HBM per device.

v0:
```python
import math
import jax
import jax.numpy as jnp
from jax import lax
from jax.sharding import PartitionSpec as P


def forward_tiles(edge_tiles, rows_at, cols_at, live_mask, column, row_tiles):
    tile_total, tile_size, _ = edge_tiles.shape
    channels = column.shape[1]
    col_blocks = column.reshape(-1, tile_size, channels)
    step_size = math.gcd(tile_total, 16)

    def forward_advance(step_index, carry):
        summed, degree = carry
        offset = step_index * step_size
        tile_group = lax.dynamic_slice_in_dim(edge_tiles, offset, step_size, 0)
        where_rows = lax.dynamic_slice_in_dim(rows_at, offset, step_size, 0)
        where_cols = lax.dynamic_slice_in_dim(cols_at, offset, step_size, 0)
        weights = lax.dynamic_slice_in_dim(live_mask, offset, step_size, 0)
        picked = col_blocks[where_cols]
        products = jnp.einsum(
            "tij,tjf->tif", tile_group, picked, preferred_element_type=jnp.float32
        )
        row_sums = jnp.sum(tile_group.astype(jnp.float32), axis=2)
        summed = summed.at[where_rows].add(products * weights[:, None, None])
        degree = degree.at[where_rows].add(row_sums * weights[:, None])
        return (summed, degree)

    start_sums = (
        jnp.zeros((row_tiles, tile_size, channels), jnp.float32),
        jnp.zeros((row_tiles, tile_size), jnp.float32),
    )
    return lax.fori_loop(0, tile_total // step_size, forward_advance, start_sums)


def backward_tiles(edge_tiles, rows_at, cols_at, live_mask, row_grads, col_tiles):
    tile_total, tile_size, _ = edge_tiles.shape
    channels = row_grads.shape[1]
    row_blocks = row_grads.reshape(-1, tile_size, channels)
    step_size = math.gcd(tile_total, 16)

    def backward_advance(step_index, summed):
        offset = step_index * step_size
        tile_group = lax.dynamic_slice_in_dim(edge_tiles, offset, step_size, 0)
        where_rows = lax.dynamic_slice_in_dim(rows_at, offset, step_size, 0)
        where_cols = lax.dynamic_slice_in_dim(cols_at, offset, step_size, 0)
        weights = lax.dynamic_slice_in_dim(live_mask, offset, step_size, 0)
        picked = row_blocks[where_rows]
        products = jnp.einsum(
            "tij,tif->tjf", tile_group, picked, preferred_element_type=jnp.float32
        )
        return summed.at[where_cols].add(products * weights[:, None, None])

    return lax.fori_loop(
        0,
        tile_total // step_size,
        backward_advance,
        jnp.zeros((col_tiles, tile_size, channels), jnp.float32),
    )


def times_transposed(left, right):
    return lax.dot_general(
        left, right, (((1,), (1,)), ((), ())), preferred_element_type=jnp.float32
    )


def shards(
    features,
    edge_tiles,
    tile_rows,
    tile_cols,
    tile_count,
    node_order,
    w_self,
    w_neigh,
    bias_term,
    cotangent,
):
    ordering = node_order[0]
    own_rows = features[ordering]
    node_dev = own_rows.shape[0]
    channels = own_rows.shape[1]
    tile_size = edge_tiles.shape[1]
    tile_total = edge_tiles.shape[0]
    col_count = lax.axis_size("col")
    row_count = lax.axis_size("row")
    live_mask = (jnp.arange(tile_total) < tile_count[0]).astype(jnp.float32)
    rows_at = tile_rows[0]
    cols_at = tile_cols[0]
    column = lax.all_gather(own_rows, "row", axis=0, tiled=True)
    summed, degree = forward_tiles(
        edge_tiles, rows_at, cols_at, live_mask, column, col_count * node_dev // tile_size
    )
    summed = summed.reshape(col_count * node_dev, channels)
    degree = degree.reshape(col_count * node_dev)
    own_sum, own_degree = (
        lax.psum_scatter(summed, "col", scatter_dimension=0, tiled=True),
        lax.psum_scatter(degree, "col", scatter_dimension=0, tiled=True),
    )
    inverse_degree = 1.0 / (1.0 + own_degree)
    neigh_mean = (own_sum * inverse_degree[:, None]).astype(jnp.bfloat16)
    preact = (
        jnp.dot(own_rows, w_self, preferred_element_type=jnp.float32)
        + jnp.dot(neigh_mean, w_neigh, preferred_element_type=jnp.float32)
        + bias_term.astype(jnp.float32)
    )
    activations = (jnp.maximum(preact, 0.0) + jnp.expm1(jnp.minimum(preact, 0.0))).astype(
        jnp.bfloat16
    )
    grad_pre = (cotangent.astype(jnp.float32) * jnp.exp(jnp.minimum(preact, 0.0))).astype(
        jnp.bfloat16
    )
    self_part = lax.dot_general(
        own_rows, grad_pre, (((0,), (0,)), ((), ())), preferred_element_type=jnp.float32
    )
    neigh_part = lax.dot_general(
        neigh_mean, grad_pre, (((0,), (0,)), ((), ())), preferred_element_type=jnp.float32
    )
    bias_part = jnp.sum(grad_pre.astype(jnp.float32), axis=0)
    self_grad, neigh_grad, bias_grad = lax.psum((self_part, neigh_part, bias_part), ("row", "col"))
    own_agg = (times_transposed(grad_pre, w_neigh) * inverse_degree[:, None]).astype(jnp.bfloat16)
    row_grads = lax.all_gather(own_agg, "col", axis=0, tiled=True)
    col_terms = backward_tiles(
        edge_tiles, rows_at, cols_at, live_mask, row_grads, row_count * node_dev // tile_size
    )
    own_grad = lax.psum_scatter(
        col_terms.reshape(row_count * node_dev, channels), "row", scatter_dimension=0, tiled=True
    )
    local_grad = times_transposed(grad_pre, w_self) + own_grad
    feature_grad = jnp.zeros_like(local_grad).at[ordering].set(local_grad)
    return (activations, feature_grad, self_grad, neigh_grad, bias_grad)


def solution(mesh):
    placed = (
        P(("row", "col"), None),
        P(("row", "col"), None, None),
        P(("row", "col"), None),
        P(("row", "col"), None),
        P(("row", "col")),
        P(("row", "col"), None),
        P(),
        P(),
        P(),
        P(("row", "col"), None),
    )
    return jax.shard_map(
        shards,
        mesh=mesh,
        in_specs=placed,
        out_specs=(P(("row", "col"), None), P(("row", "col"), None), P(), P(), P()),
        check_vma=False,
    )
```

profile of v0, /device:TPU:2, one launch (start us, length us, event | category | flops | bytes accessed | tf_op | source)
XLA Modules:
  0.0 742.1 jit_solution(8785978623316834144)
XLA Ops:
  7.2 0.7 fusion.11
  7.9 2.4 gather_fusion.2
  11.1 64.9 %all-gather.6.cloned.1.call-done = bf16[4096,512]{1,0:T(8,128)(2,1)} async-done(((bf16[128,512]{1,0:T(8,128)(2,1)}), bf16[4096,512]{1,0:T(8,128)(2,1)}) %all-gather.6.cloned.1.call-update) | async-done | bytes 4194320 | tf_op jit(solution)/shard_map/all_gather | solution.py:92
  76.0 0.2 broadcast_in_dim.52
  76.3 35.4 %while.28 = (s32[]{:T(128)}, f32[8,128,512]{2,1,0:T(8,128)S(1)}, f32[8,128]{1,0:T(8,128)S(1)}, s32[32]{0:T(128)}, bf16[32,128,128]{2,1,0:T(8,128)(2,1)}, /*index...) while((s32[]{:T(128)}, f32[8,128,512]{2,1,0:T(8,128)S(1)}, ...), condition=%wide.region_4.0_spmd, body=%wide.region_0.0_spmd.sunk | while | flops 271060064 | bytes 24143164 | solution.py:34
  76.4 0.8 compare_select_fusion.7
  77.2 4.3 gather_fusion
  81.4 0.1 dynamic_slice.75
  81.5 4.4 convolution_multiply_fusion.5
  85.9 6.1 scatter_fusion
  92.1 1.3 convert_reduce_fusion.3
  93.4 0.7 scatter_custom_fusion.12
  94.1 0.8 compare_select_fusion.7
  94.8 4.3 gather_fusion
  99.2 4.4 convolution_multiply_fusion.5
  103.6 6.1 scatter_fusion
  109.8 1.3 convert_reduce_fusion.3
  111.0 0.7 scatter_custom_fusion.12
  111.7 1.3 copy-done.1
  113.2 0.6 dynamic-slice
  114.5 0.2 fusion.14
  114.7 28.1 %all-reduce = f32[1024]{0:T(1024)S(1)} all-reduce(f32[1024]{0:T(1024)S(1)} %bitcast.36), channel_id=4, replica_groups=mesh['row'=32,'col'=8] {'col'}, use_global_device_ids=true, to_apply=%region_6.0.clone | all-reduce | flops 1024 | bytes 8192
  142.8 0.1 fusion.12
  142.9 65.3 %reduce-scatter.3.cloned.1.call-done = f32[128,512]{1,0:T(8,128)} async-done(((f32[1024,512]{1,0:T(8,128)}), f32[128,512]{1,0:T(8,128)}) %reduce-scatter.3.cloned.1.call-update) | async-done | bytes 262160 | tf_op jit(solution)/shard_map/reduce_scatter | solution.py:99
  208.2 2.0 convert_reduce_fusion.1
  210.2 1.0 fusion.8
  211.3 57.7 %all-gather.4.cloned.1.call-done = bf16[1024,512]{1,0:T(8,128)(2,1)} async-done(((bf16[128,512]{1,0:T(8,128)(2,1)}), bf16[1024,512]{1,0:T(8,128)(2,1)}) %all-gather.4.cloned.1.call-update) | async-done | bytes 1048592 | tf_op jit(solution)/shard_map/all_gather | solution.py:124
  269.0 4.3 broadcast_in_dim.54
  273.2 31.1 %while.29 = (s32[]{:T(128)}, f32[32,128,512]{2,1,0:T(8,128)}, s32[32]{0:T(128)S(1)}, bf16[32,128,128]{2,1,0:T(8,128)(2,1)}, s32[32]{0:T(128)S(1)}, /*index=5*/bf...) while((s32[]{:T(128)}, f32[32,128,512]{2,1,0:T(8,128)}, ...), condition=%wide.region_9.0_spmd, body=%wide.region_7.9_spmd.sunk | while | flops 270533728 | bytes 23597872 | solution.py:55
  273.2 0.1 compare_select_fusion.8
  273.3 1.9 gather_fusion.1
  275.2 0.1 dynamic_slice.78
  275.3 3.9 convolution_multiply_fusion.6
  279.2 9.6 %scatter_fusion.1 = f32[32,128,512]{2,1,0:T(8,128)} fusion(f32[32,128,512]{2,1,0:T(8,128)} %get-tuple-element.473, s32[16]{0:T(128)S(1)} %get-tuple-element.423, f32[16,128,512]{2,1,0:T(8,128)} %convolution_multiply_fusion.6), kind=kCustom, calls=%fused_computation.5.clone.1 | custom fusion | flops 1048576 | bytes 12582976 | tf_op jit(solution)/shard_map/while/body/eval_jaxpr/scatter-add | solution.py:53
  288.8 0.1 compare_select_fusion.8
  288.9 1.9 gather_fusion.1
  290.8 0.1 dynamic_slice.78
  290.9 3.9 convolution_multiply_fusion.6
  294.7 9.6 %scatter_fusion.1 = f32[32,128,512]{2,1,0:T(8,128)} fusion(f32[32,128,512]{2,1,0:T(8,128)} %get-tuple-element.473, s32[16]{0:T(128)S(1)} %get-tuple-element.423, f32[16,128,512]{2,1,0:T(8,128)} %convolution_multiply_fusion.6), kind=kCustom, calls=%fused_computation.5.clone.1 | custom fusion | flops 1048576 | bytes 12582976 | tf_op jit(solution)/shard_map/while/body/eval_jaxpr/scatter-add | solution.py:53
  304.4 1.3 fusion.15
  305.7 1.4 fusion.13
  307.1 74.2 %psum.23 = f32[512]{0:T(512)} all-reduce(f32[512]{0:T(512)S(1)} %get-tuple-element.318), channel_id=1, replica_groups=mesh['row'=32,'col'=8] {'row','col'}, use_global_device_ids=true, to_apply=%region_15.0 | all-reduce | flops 512 | bytes 4096 | tf_op jit(solution)/shard_map/psum | solution.py:122
  381.3 83.5 %reduce-scatter.5.cloned.1.call-done = f32[128,512]{1,0:T(8,128)} async-done(((f32[4096,512]{1,0:T(8,128)}), f32[128,512]{1,0:T(8,128)}) %reduce-scatter.5.cloned.1.call-update) | async-done | bytes 262160 | tf_op jit(solution)/shard_map/reduce_scatter | solution.py:128
  464.8 1.2 convolution_add_fusion
  466.0 1.7 scatter_custom_fusion.3
  467.7 263.4 %all-reduce.4.cloned.1.call-done = (f32[512,512]{1,0:T(8,128)}, f32[512,512]{1,0:T(8,128)}) async-done(((f32[512,512]{1,0:T(8,128)}, f32[512,512]{1,0:T(8,128)}), (f32[512,512]{1,0:T(8,128)}, f32[512,512]{1,0:T(8,128)})) %all-reduce.4.cloned.1.call-update) | async-done | bytes 2097168 | tf_op jit(solution)/shard_map/psum | solution.py:122
  731.1 2.3 copy.39
  733.4 2.3 copy.40
  (38 shorter events, 0.5 us)
Async XLA Ops:
  7.2 201.1 %copy-start = (bf16[512,512]{1,0:T(8,128)(2,1)S(1)}, bf16[512,512]{1,0:T(8,128)(2,1)}, u32[]{:S(2)}) copy-start(bf16[512,512]{1,0:T(8,128)(2,1)} %param.21) | copy-start | bytes 1572868
  7.2 68.8 %all-gather.6.cloned.1.call-start = ((), (), s32[]{:S(2)}) async-start(), calls=%async_computation.5 | async-start | bytes 4325376 | tf_op jit(solution)/shard_map/all_gather | solution.py:92
  10.4 197.8 %reduce-scatter.3.cloned.1.call-start = ((), (), s32[]{:S(2)}) async-start(), calls=%async_computation.2 | async-start | bytes 2359296 | tf_op jit(solution)/shard_map/reduce_scatter | solution.py:99
  76.3 36.9 %copy-start.8 = (bf16[512]{0:T(512)(128)(2,1)S(1)}, bf16[512]{0:T(512)(128)(2,1)}, u32[]{:S(2)}) copy-start(bf16[512]{0:T(512)(128)(2,1)} %param.22) | copy-start | bytes 3076
  76.3 36.9 %copy-start.9 = (u32[256]{0:T(256)S(1)}, u32[256]{0:T(256)}, u32[]{:S(2)}) copy-start(u32[256]{0:T(256)} %constant.100) | copy-start | bytes 3076
  76.3 38.1 %copy-start.2 = (bf16[128,512]{1,0:T(8,128)(2,1)S(1)}, bf16[128,512]{1,0:T(8,128)(2,1)}, u32[]{:S(2)}) copy-start(bf16[128,512]{1,0:T(8,128)(2,1)} %gather_fusion.2) | copy-start | bytes 393220
  76.3 38.1 %copy-start.3 = (bf16[512,512]{1,0:T(8,128)(2,1)S(1)}, bf16[512,512]{1,0:T(8,128)(2,1)}, u32[]{:S(2)}) copy-start(bf16[512,512]{1,0:T(8,128)(2,1)} %param.20) | copy-start | bytes 1572868
  76.3 131.9 %copy-start.5 = (bf16[128,512]{1,0:T(8,128)(2,1)S(1)}, bf16[128,512]{1,0:T(8,128)(2,1)}, u32[]{:S(2)}) copy-start(bf16[128,512]{1,0:T(8,128)(2,1)} %param.23) | copy-start | bytes 393220
  111.7 1.3 copy-start.1
  113.1 155.8 %all-gather.4.cloned.1.call-start = ((), (), s32[]{:S(2)}) async-start(), calls=%async_computation.3 | async-start | bytes 1179648 | tf_op jit(solution)/shard_map/all_gather | solution.py:124
  211.2 253.6 %reduce-scatter.5.cloned.1.call-start = ((), (), s32[]{:S(2)}) async-start(), calls=%async_computation.4 | async-start | bytes 8650752 | tf_op jit(solution)/shard_map/reduce_scatter | solution.py:128
  268.9 4.3 copy-start.6
  268.9 4.3 copy-start.7
  304.4 1.4 copy-start.4
  304.4 426.7 %all-reduce.4.cloned.1.call-start = ((), (), s32[]{:S(2)}) async-start(), calls=%async_computation.6 | async-start | bytes 4194304 | tf_op jit(solution)/shard_map/psum | solution.py:122
Sparse Core Ops, SparseCore 0:
  10.5 65.4 all-gather.5
  113.2 94.9 reduce-scatter.2
  211.4 57.4 all-gather.3
  304.5 160.2 reduce-scatter.4
  470.7 260.2 all-reduce.3
where the time goes:
time: 743 us; the launch traced here: 742 us
  waiting for transfers between devices  535 us (72%)
  blocking collectives  102 us (14%)
  other arithmetic  38 us (5%)
  local copies, waits for them, and re-layouts  27.8 us (4%)
  matrix products  23.6 us (3%)
  between operations  15.2 us (2%)
    psum x1, waiting for transfers between devices, shards(): lax.psum((self_part, neigh_part, bias_part), ('row', 'col'))  263 us
    reduce_scatter x1, waiting for transfers between devices, shards(): lax.psum_scatter(col_terms.reshape(row_count * node_dev, channels), 'row'...  83.5 us
    psum x1, blocking collectives, shards(): lax.psum((self_part, neigh_part, bias_part), ('row', 'col'))  74.2 us
    reduce_scatter x1, waiting for transfers between devices, shards(): lax.psum_scatter(summed, 'col', scatter_dimension=0, tiled=True)  65.3 us
    all_gather x1, waiting for transfers between devices, shards(): column = lax.all_gather(own_rows, 'row', axis=0, tiled=True)  64.9 us
    all_gather x1, waiting for transfers between devices, shards(): row_grads = lax.all_gather(own_agg, 'col', axis=0, tiled=True)  57.7 us
    unnamed x1, blocking collectives  28.1 us
    scatter-add x2, other arithmetic, backward_advance(): return summed.at[where_cols].add(products * weights[:, None, None])  19.3 us
  transfers between devices with their start and end apart: 5, of which 5 were waited for; matrix products, arithmetic and copies ran while one was open for 1% of the time, Pallas kernels for 0%

commit v1 on v0

--- a/solution.py
+++ b/solution.py
@@ -121,7 +121,9 @@
     bias_part = jnp.sum(grad_pre.astype(jnp.float32), axis=0)
     self_grad, neigh_grad, bias_grad = lax.psum((self_part, neigh_part, bias_part), ("row", "col"))
     own_agg = (times_transposed(grad_pre, w_neigh) * inverse_degree[:, None]).astype(jnp.bfloat16)
-    row_grads = lax.all_gather(own_agg, "col", axis=0, tiled=True)
+    row_grads = jnp.concatenate(
+        lax.all_to_all(jnp.stack([own_agg] * lax.axis_size("col")), "col", 0, 0), axis=0
+    )
     col_terms = backward_tiles(
         edge_tiles, rows_at, cols_at, live_mask, row_grads, row_count * node_dev // tile_size
     )

time: 743 us -> 720 us (0.969)
  waiting for transfers between devices: 535 us -> 502 us
    all_gather x1 -> x0, waiting for transfers between devices: 57.7 us -> none  [shards(): row_grads = lax.all_gather(own_agg, 'col', axis=0, tiled=True)]
    all_to_all x0 -> x1, waiting for transfers between devices: none -> 26.4 us  [shards(): lax.all_to_all(jnp.stack([own_agg] * lax.axis_size('col')), 'col', 0, 0)]
where the time goes in v1:
time: 720 us; the launch traced here: 719 us
  waiting for transfers between devices  502 us (70%)
  blocking collectives  105 us (15%)
  other arithmetic  38 us (5%)
  local copies, waits for them, and re-layouts  30.6 us (4%)
  matrix products  22.9 us (3%)
  between operations  15.2 us (2%)
    psum x1, waiting for transfers between devices, shards(): lax.psum((self_part, neigh_part, bias_part), ('row', 'col'))  264 us
    reduce_scatter x1, waiting for transfers between devices, shards(): lax.psum_scatter(col_terms.reshape(row_count * node_dev, channels), 'row'...  80.7 us
    psum x1, blocking collectives, shards(): lax.psum((self_part, neigh_part, bias_part), ('row', 'col'))  77.2 us
    reduce_scatter x1, waiting for transfers between devices, shards(): lax.psum_scatter(summed, 'col', scatter_dimension=0, tiled=True)  65.3 us
    all_gather x1, waiting for transfers between devices, shards(): column = lax.all_gather(own_rows, 'row', axis=0, tiled=True)  64.9 us
    unnamed x1, blocking collectives  28.1 us
    all_to_all x1, waiting for transfers between devices, shards(): lax.all_to_all(jnp.stack([own_agg] * lax.axis_size('col')), 'col', 0, 0)  26.4 us
    scatter-add x2, other arithmetic, backward_advance(): return summed.at[where_cols].add(products * weights[:, None, None])  19.2 us
  transfers between devices with their start and end apart: 5, of which 5 were waited for; matrix products, arithmetic and copies ran while one was open for 1% of the time, Pallas kernels for 0%

profile of v1, /device:TPU:2, one launch (start us, length us, event | category | flops | bytes accessed | tf_op | source)
XLA Modules:
  0.0 718.7 jit_solution(7224226879735413189)
XLA Ops:
  7.2 0.7 fusion.11
  7.9 2.4 gather_fusion.2
  11.1 64.9 %all-gather.3.cloned.1.call-done = bf16[4096,512]{1,0:T(8,128)(2,1)} async-done(((bf16[128,512]{1,0:T(8,128)(2,1)}), bf16[4096,512]{1,0:T(8,128)(2,1)}) %all-gather.3.cloned.1.call-update) | async-done | bytes 4194320 | tf_op jit(solution)/shard_map/all_gather | solution.py:92
  76.0 0.2 broadcast_in_dim.52
  76.3 35.3 %while.28 = (s32[]{:T(128)}, f32[8,128,512]{2,1,0:T(8,128)S(1)}, f32[8,128]{1,0:T(8,128)S(1)}, s32[32]{0:T(128)}, bf16[32,128,128]{2,1,0:T(8,128)(2,1)}, /*index...) while((s32[]{:T(128)}, f32[8,128,512]{2,1,0:T(8,128)S(1)}, ...), condition=%wide.region_4.0_spmd, body=%wide.region_0.0_spmd.sunk | while | flops 271060064 | bytes 24143164 | solution.py:34
  76.4 0.8 compare_select_fusion.7
  77.2 4.2 gather_fusion
  81.5 4.4 convolution_multiply_fusion.5
  85.9 6.1 scatter_fusion
  92.1 1.3 convert_reduce_fusion.3
  93.3 0.7 scatter_custom_fusion.12
  94.1 0.8 compare_select_fusion.7
  94.8 4.2 gather_fusion
  99.1 4.4 convolution_multiply_fusion.5
  103.6 6.1 scatter_fusion
  109.7 1.3 convert_reduce_fusion.3
  111.0 0.7 scatter_custom_fusion.12
  111.7 1.3 copy-done.1
  113.1 0.6 dynamic-slice
  114.4 0.2 fusion.14
  114.6 28.1 %all-reduce = f32[1024]{0:T(1024)S(1)} all-reduce(f32[1024]{0:T(1024)S(1)} %bitcast.34), channel_id=4, replica_groups=mesh['row'=32,'col'=8] {'col'}, use_global_device_ids=true, to_apply=%region_6.0.clone | all-reduce | flops 1024 | bytes 8192
  142.7 0.1 fusion.12
  142.8 65.3 %reduce-scatter.3.cloned.1.call-done = f32[128,512]{1,0:T(8,128)} async-done(((f32[1024,512]{1,0:T(8,128)}), f32[128,512]{1,0:T(8,128)}) %reduce-scatter.3.cloned.1.call-update) | async-done | bytes 262160 | tf_op jit(solution)/shard_map/reduce_scatter | solution.py:99
  208.1 2.0 convert_reduce_fusion.1
  210.1 0.3 fusion.8
  210.4 1.1 stack.2
  211.4 4.5 all-to-all-start
  216.0 26.4 %all-to-all-done = bf16[8,128,512]{2,1,0:T(8,128)(2,1)S(1)} async-done(((bf16[8,128,512]{2,1,0:T(8,128)(2,1)}), bf16[8,128,512]{2,1,0:T(8,128)(2,1)S(1)}, u32[]{:S(2)}, u32[]{:S(2)}) %all-to-all-start) | async-done | bytes 1048608 | tf_op jit(solution)/shard_map/all_to_all | solution.py:125
  242.4 4.3 broadcast_in_dim.54
  246.7 32.8 %while.29 = (s32[]{:T(128)}, f32[32,128,512]{2,1,0:T(8,128)}, s32[32]{0:T(128)S(1)}, bf16[32,128,128]{2,1,0:T(8,128)(2,1)}, s32[32]{0:T(128)S(1)}, /*index=5*/bf...) while((s32[]{:T(128)}, f32[32,128,512]{2,1,0:T(8,128)}, ...), condition=%wide.region_9.0_spmd, body=%wide.region_7.9_spmd.sunk | while | flops 270533728 | bytes 31986536 | solution.py:55
  246.8 0.9 copy-done.2
  247.7 1.9 gather_fusion.1
  249.6 0.1 dynamic_slice.78
  249.7 3.8 convolution_multiply_fusion.6
  253.5 9.6 %scatter_fusion.1 = f32[32,128,512]{2,1,0:T(8,128)} fusion(f32[32,128,512]{2,1,0:T(8,128)} %get-tuple-element.473, s32[16]{0:T(128)S(1)} %get-tuple-element.423, f32[16,128,512]{2,1,0:T(8,128)} %convolution_multiply_fusion.6), kind=kCustom, calls=%fused_computation.5.clone.1 | custom fusion | flops 1048576 | bytes 12582976 | tf_op jit(solution)/shard_map/while/body/eval_jaxpr/scatter-add | solution.py:53
  263.2 0.9 copy-done.2
  264.1 1.9 gather_fusion.1
  266.1 3.8 convolution_multiply_fusion.6
  269.9 9.6 %scatter_fusion.1 = f32[32,128,512]{2,1,0:T(8,128)} fusion(f32[32,128,512]{2,1,0:T(8,128)} %get-tuple-element.473, s32[16]{0:T(128)S(1)} %get-tuple-element.423, f32[16,128,512]{2,1,0:T(8,128)} %convolution_multiply_fusion.6), kind=kCustom, calls=%fused_computation.5.clone.1 | custom fusion | flops 1048576 | bytes 12582976 | tf_op jit(solution)/shard_map/while/body/eval_jaxpr/scatter-add | solution.py:53
  279.6 1.3 fusion.15
  280.9 1.4 fusion.13
  282.3 77.2 %psum.23 = f32[512]{0:T(512)} all-reduce(f32[512]{0:T(512)S(1)} %get-tuple-element.318), channel_id=1, replica_groups=mesh['row'=32,'col'=8] {'row','col'}, use_global_device_ids=true, to_apply=%region_15.0 | all-reduce | flops 512 | bytes 4096 | tf_op jit(solution)/shard_map/psum | solution.py:122
  359.6 80.7 %reduce-scatter.5.cloned.1.call-done = f32[128,512]{1,0:T(8,128)} async-done(((f32[4096,512]{1,0:T(8,128)}), f32[128,512]{1,0:T(8,128)}) %reduce-scatter.5.cloned.1.call-update) | async-done | bytes 262160 | tf_op jit(solution)/shard_map/reduce_scatter | solution.py:130
  440.3 1.3 convolution_add_fusion
  441.5 1.7 scatter_custom_fusion.3
  443.2 264.4 %all-reduce.4.cloned.1.call-done = (f32[512,512]{1,0:T(8,128)}, f32[512,512]{1,0:T(8,128)}) async-done(((f32[512,512]{1,0:T(8,128)}, f32[512,512]{1,0:T(8,128)}), (f32[512,512]{1,0:T(8,128)}, f32[512,512]{1,0:T(8,128)})) %all-reduce.4.cloned.1.call-update) | async-done | bytes 2097168 | tf_op jit(solution)/shard_map/psum | solution.py:122
  707.7 2.3 copy.39
  709.9 2.3 copy.40
  (46 shorter events, 0.7 us)
Async XLA Ops:
  7.2 200.9 %copy-start = (bf16[512,512]{1,0:T(8,128)(2,1)S(1)}, bf16[512,512]{1,0:T(8,128)(2,1)}, u32[]{:S(2)}) copy-start(bf16[512,512]{1,0:T(8,128)(2,1)} %param.21) | copy-start | bytes 1572868
  7.2 68.8 %all-gather.3.cloned.1.call-start = ((), (), s32[]{:S(2)}) async-start(), calls=%async_computation.5 | async-start | bytes 4325376 | tf_op jit(solution)/shard_map/all_gather | solution.py:92
  10.4 197.6 %reduce-scatter.3.cloned.1.call-start = ((), (), s32[]{:S(2)}) async-start(), calls=%async_computation.3 | async-start | bytes 2359296 | tf_op jit(solution)/shard_map/reduce_scatter | solution.py:99
  76.3 36.8 %copy-start.10 = (bf16[512]{0:T(512)(128)(2,1)S(1)}, bf16[512]{0:T(512)(128)(2,1)}, u32[]{:S(2)}) copy-start(bf16[512]{0:T(512)(128)(2,1)} %param.22) | copy-start | bytes 3076
  76.3 36.8 %copy-start.11 = (u32[256]{0:T(256)S(1)}, u32[256]{0:T(256)}, u32[]{:S(2)}) copy-start(u32[256]{0:T(256)} %constant.100) | copy-start | bytes 3076
  76.3 38.0 %copy-start.4 = (bf16[128,512]{1,0:T(8,128)(2,1)S(1)}, bf16[128,512]{1,0:T(8,128)(2,1)}, u32[]{:S(2)}) copy-start(bf16[128,512]{1,0:T(8,128)(2,1)} %gather_fusion.2) | copy-start | bytes 393220
  76.3 38.0 %copy-start.5 = (bf16[512,512]{1,0:T(8,128)(2,1)S(1)}, bf16[512,512]{1,0:T(8,128)(2,1)}, u32[]{:S(2)}) copy-start(bf16[512,512]{1,0:T(8,128)(2,1)} %param.20) | copy-start | bytes 1572868
  76.3 131.7 %copy-start.7 = (bf16[128,512]{1,0:T(8,128)(2,1)S(1)}, bf16[128,512]{1,0:T(8,128)(2,1)}, u32[]{:S(2)}) copy-start(bf16[128,512]{1,0:T(8,128)(2,1)} %param.23) | copy-start | bytes 393220
  111.7 1.3 copy-start.1
  211.4 31.0 %all-to-all-start = ((bf16[8,128,512]{2,1,0:T(8,128)(2,1)}), bf16[8,128,512]{2,1,0:T(8,128)(2,1)S(1)}, u32[]{:S(2)}, u32[]{:S(2)}) async-start(bf16[8,128,512]{2,1,0:T(8,128)(2,1)} %stack.2), calls=%async_computation.1 | async-start | bytes 2097152 | tf_op jit(solution)/shard_map/all_to_all | solution.py:125
  216.0 224.3 %reduce-scatter.5.cloned.1.call-start = ((), (), s32[]{:S(2)}) async-start(), calls=%async_computation.4 | async-start | bytes 8650752 | tf_op jit(solution)/shard_map/reduce_scatter | solution.py:130
  216.0 30.7 %copy-start.8 = (s32[32]{0:T(128)S(1)}, s32[32]{0:T(128)}, u32[]{:S(2)}) copy-start(s32[32]{0:T(128)} %get-tuple-element.523) | copy-start | bytes 388
  216.0 30.7 %copy-start.9 = (s32[32]{0:T(128)S(1)}, s32[32]{0:T(128)}, u32[]{:S(2)}) copy-start(s32[32]{0:T(128)} %get-tuple-element.524) | copy-start | bytes 388
  246.7 1.0 copy-start.2
  253.5 9.6 %copy-start.3 = (bf16[8,128,512]{2,1,0:T(8,128)(2,1)S(1)}, bf16[8,128,512]{2,1,0:T(8,128)(2,1)}, u32[]{:S(2)}) copy-start(bf16[8,128,512]{2,1,0:T(8,128)(2,1)} %copy-done.2) | copy-start | bytes 3145732 | tf_op jit(solution)/shard_map/while
  263.1 1.0 copy-start.2
  269.9 9.6 %copy-start.3 = (bf16[8,128,512]{2,1,0:T(8,128)(2,1)S(1)}, bf16[8,128,512]{2,1,0:T(8,128)(2,1)}, u32[]{:S(2)}) copy-start(bf16[8,128,512]{2,1,0:T(8,128)(2,1)} %copy-done.2) | copy-start | bytes 3145732 | tf_op jit(solution)/shard_map/while
  279.6 1.4 copy-start.6
  279.6 428.1 %all-reduce.4.cloned.1.call-start = ((), (), s32[]{:S(2)}) async-start(), calls=%async_computation.6 | async-start | bytes 4194304 | tf_op jit(solution)/shard_map/psum | solution.py:122
Sparse Core Ops, SparseCore 0:
  10.5 65.4 all-gather.2
  113.2 94.8 reduce-scatter.2
  279.7 160.5 reduce-scatter.4
  446.3 261.3 all-reduce.3
